TPU v7x, 32 devices: a whole 2x2x4 slice. The times are simulated.
32 devices in a mesh: shard: 4 (over y, x), ctx: 4 (over z), tp: 2 (over core).
Axes of the slice: x: 2, y: 2, z: 4, core: 2. Of those that a mesh axis runs over, the one named last changes fastest.
Arguments:
- inputs: bfloat16 [4, 512, 1024], P('shard', 'ctx'), may hold values from -6 to 6
- cotangent: bfloat16 [4, 512, 1024], P('shard', 'ctx'), may hold values from -6 to 6
- mixer_matrix: float32 [1024, 4, 1024], P(('shard', 'ctx', 'tp')), may hold values from -0.1875 to 0.1875
- ffn_weight: float32 [4608, 3, 1024], P(('shard', 'ctx', 'tp')), may hold values from -0.1875 to 0.1875
- conv_weight: float32 [3, 1024], replicated, may hold values from -3.5 to 3.5
- norm_gains: float32 [2, 1024], replicated, may hold values from 0.5 to 1.5
- mixer_first: float32 [1024, 4, 1024], P(('shard', 'ctx', 'tp')), as said below
- mixer_second: float32 [1024, 4, 1024], P(('shard', 'ctx', 'tp')), as said below
- ffn_first: float32 [4608, 3, 1024], P(('shard', 'ctx', 'tp')), as said below
- ffn_second: float32 [4608, 3, 1024], P(('shard', 'ctx', 'tp')), as said below
- conv_first: float32 [3, 1024], replicated, as said below
- conv_second: float32 [3, 1024], replicated, as said below
- gain_first: float32 [2, 1024], replicated, as said below
- gain_second: float32 [2, 1024], replicated, as said below
Outputs:
- output: bfloat16 [4, 512, 1024], P('shard', 'ctx')
- input_grad: float32 [4, 512, 1024], P('shard', 'ctx')
- mixer_grad: float32 [1024, 4, 1024], P(('shard', 'ctx', 'tp'))
- ffn_grad: float32 [4608, 3, 1024], P(('shard', 'ctx', 'tp'))
- conv_grad: float32 [3, 1024], replicated
- gain_grad: float32 [2, 1024], replicated
- mixer_new: float32 [1024, 4, 1024], P(('shard', 'ctx', 'tp'))
- ffn_new: float32 [4608, 3, 1024], P(('shard', 'ctx', 'tp'))
- conv_new: float32 [3, 1024], replicated
- gain_new: float32 [2, 1024], replicated
- mixer_first_new: float32 [1024, 4, 1024], P(('shard', 'ctx', 'tp'))
- mixer_second_new: float32 [1024, 4, 1024], P(('shard', 'ctx', 'tp'))
- ffn_first_new: float32 [4608, 3, 1024], P(('shard', 'ctx', 'tp'))
- ffn_second_new: float32 [4608, 3, 1024], P(('shard', 'ctx', 'tp'))
- conv_first_new: float32 [3, 1024], replicated
- conv_second_new: float32 [3, 1024], replicated
- gain_first_new: float32 [2, 1024], replicated
- gain_second_new: float32 [2, 1024], replicated
Inputs may be any that keep to these rules, and one draw needn't show every extreme that they name: `mixer_first`: a running mean of earlier gradients. `mixer_second`: a running mean of squared earlier gradients. `ffn_first`: a running mean of earlier gradients. `ffn_second`: a running mean of squared earlier gradients. `conv_first`: a running mean of earlier gradients. `conv_second`: a running mean of squared earlier gradients. `gain_first`: a running mean of earlier gradients. `gain_second`: a running mean of squared earlier gradients.
All inputs are finite; a program needn't handle non-finite values.
Results may differ from a plain program's by a relative error of at most 0.009.
The roundings to bfloat16 on the way count: a program that leaves them out, or rounds other values in their place, can miss the bound.
Values may be sent and summed in bfloat16 or wider, within the bound.
No kernel may reach another device: no remote copies, remote signals or barrier semaphores. Data moves between devices by JAX's collectives and lax.ppermute only.
A program may use at most 192 MiB of HBM per device.

v0:
```python
import jax
import jax.numpy as jnp
from jax import lax
from jax.sharding import PartitionSpec as P

STEP = 10
norm_eps = 1e-05
beta_first = 0.9
beta_second = 0.999
adam_eps = 1e-08
matrix_rate = 0.02
small_rate = 0.25
decay_rate = 0.1


def shifted(value, axis, steps):
    count = lax.axis_size(axis)
    leading, last = (max(0, -steps), min(count, count - steps))
    return lax.ppermute(value, axis, [(source, source + steps) for source in range(leading, last)])


def rms_scale(values):
    return lax.rsqrt(jnp.mean(values * values, axis=-1, keepdims=True) + norm_eps)


def norm_backward(grad_normed, normed, scale):
    return scale * (grad_normed - normed * jnp.mean(grad_normed * normed, axis=-1, keepdims=True))


def adam_update(weight, gradient, first, second, rate, decay):
    first_new = beta_first * first + (1.0 - beta_first) * gradient
    second_new = beta_second * second + (1.0 - beta_second) * gradient * gradient
    first_hat = first_new / (1.0 - beta_first**STEP)
    second_hat = second_new / (1.0 - beta_second**STEP)
    weight_new = weight - rate * (first_hat / (jnp.sqrt(second_hat) + adam_eps) + decay * weight)
    return (weight_new, first_new, second_new)


def group_layout(model_width):
    tp_count = lax.axis_size("tp")
    group_count = lax.axis_size("shard") * lax.axis_size("ctx")
    return (tp_count, group_count, model_width // (group_count * tp_count))


def own_taps(conv_weight):
    tp_count, group_count, block_size = group_layout(conv_weight.shape[1])
    grouped = conv_weight.reshape(3, group_count, tp_count, block_size)
    picked = lax.dynamic_index_in_dim(grouped, lax.axis_index("tp"), axis=2, keepdims=False)
    return picked.reshape(3, group_count * block_size)


def spread_taps(tap_grads, model_width):
    tp_count, group_count, block_size = group_layout(model_width)
    blank_grid = jnp.zeros((3, group_count, tp_count, block_size), jnp.float32)
    placed = lax.dynamic_update_index_in_dim(
        blank_grid, tap_grads.reshape(3, group_count, block_size), lax.axis_index("tp"), 2
    )
    return placed.reshape(3, model_width)


def reduce_terms(inner_term, outer_term):
    moved_in, moved_out = (
        lax.all_to_all(
            inner_term[None].astype(jnp.bfloat16),
            ("shard", "ctx"),
            split_axis=1,
            concat_axis=0,
            tiled=True,
        ).astype(jnp.float32),
        lax.all_to_all(
            outer_term[None].astype(jnp.bfloat16),
            ("shard", "ctx"),
            split_axis=1,
            concat_axis=0,
            tiled=True,
        ).astype(jnp.float32),
    )
    summed_in = jnp.sum(moved_in, axis=0)
    summed_out = jnp.sum(moved_out, axis=0)
    return jnp.concatenate([summed_in, summed_out[:, None, :]], axis=1)


def per_device(
    inputs,
    cotangent,
    mixer_matrix,
    ffn_weight,
    conv_weight,
    norm_gains,
    mixer_first,
    mixer_second,
    ffn_first,
    ffn_second,
    conv_first,
    conv_second,
    gain_first,
    gain_second,
):
    seq_count, tok_count, model_width = inputs.shape
    row_count = seq_count * tok_count
    mixer_half = mixer_matrix.astype(jnp.bfloat16)
    ffn_half = ffn_weight.astype(jnp.bfloat16)
    mixer_whole, ffn_whole = (
        lax.all_gather(mixer_half, ("shard", "ctx"), axis=0, tiled=True),
        lax.all_gather(ffn_half, ("shard", "ctx"), axis=0, tiled=True),
    )
    channel_count = mixer_whole.shape[0]
    x_rows = inputs.reshape(row_count, model_width).astype(jnp.float32)
    scale_one = rms_scale(x_rows)
    normed_one = x_rows * scale_one
    h_one = (normed_one * norm_gains[0]).astype(jnp.bfloat16)
    h_seqs = h_one.reshape(seq_count, tok_count, model_width)
    before = shifted(h_seqs[:, tok_count - 2 :, :], "ctx", 1)
    fwd_rows = jnp.concatenate([before, h_seqs], axis=1).reshape(
        seq_count * (tok_count + 2), model_width
    )
    taps_own = own_taps(conv_weight)
    projected = jnp.einsum(
        "rd,ckd->rkc", fwd_rows, mixer_whole[:, :3, :], preferred_element_type=jnp.float32
    )
    projected = projected.reshape(seq_count, tok_count + 2, 3, channel_count)
    in_b = projected[:, :, 0, :]
    in_x = projected[:, :, 2, :]
    in_c = projected[:, 2:, 1, :]
    product = in_b * in_x
    mixed_rows = (
        taps_own[0] * product[:, :tok_count]
        + taps_own[1] * product[:, 1 : tok_count + 1]
        + taps_own[2] * product[:, 2:]
    )
    gated_row_block = (in_c * mixed_rows).astype(jnp.bfloat16).reshape(row_count, channel_count)
    mix_part = jnp.dot(gated_row_block, mixer_whole[:, 3, :], preferred_element_type=jnp.float32)
    mix_out = lax.psum(mix_part, "tp")
    residual = x_rows + mix_out
    scale_two = rms_scale(residual)
    normed_two = residual * scale_two
    h_two = (normed_two * norm_gains[1]).astype(jnp.bfloat16)
    gate_and_lift = jnp.einsum(
        "rd,ckd->rkc", h_two, ffn_whole[:, :2, :], preferred_element_type=jnp.float32
    )
    gate_pre = gate_and_lift[:, 0, :]
    up_value = gate_and_lift[:, 1, :]
    sigmoid_gate = jax.nn.sigmoid(gate_pre)
    gate_act = gate_pre * sigmoid_gate
    hidden = (gate_act * up_value).astype(jnp.bfloat16)
    ffn_part = jnp.dot(hidden, ffn_whole[:, 2, :], preferred_element_type=jnp.float32)
    ffn_out = lax.psum(ffn_part.astype(jnp.bfloat16), "tp").astype(jnp.float32)
    output = (residual + ffn_out).astype(jnp.bfloat16).reshape(inputs.shape)
    mixer_backward, ffn_back = (
        lax.all_gather(mixer_half, ("shard", "ctx"), axis=0, tiled=True),
        lax.all_gather(ffn_half, ("shard", "ctx"), axis=0, tiled=True),
    )
    grad_rows = cotangent.reshape(row_count, model_width)
    grad_float = grad_rows.astype(jnp.float32)
    grad_hidden = jnp.einsum(
        "rd,cd->rc", grad_rows, ffn_back[:, 2, :], preferred_element_type=jnp.float32
    )
    grad_gate = (
        grad_hidden * up_value * sigmoid_gate * (1.0 + gate_pre * (1.0 - sigmoid_gate))
    ).astype(jnp.bfloat16)
    grad_up = (grad_hidden * gate_act).astype(jnp.bfloat16)
    grad_pair = jnp.stack([grad_gate, grad_up], axis=1)
    part_two = jnp.einsum(
        "rkc,ckd->rd", grad_pair, ffn_back[:, :2, :], preferred_element_type=jnp.float32
    )
    grad_h_two = lax.psum(part_two, "tp")
    ffn_inner = jnp.einsum("rkc,rd->ckd", grad_pair, h_two, preferred_element_type=jnp.float32)
    ffn_outer = jnp.einsum("rc,rd->cd", hidden, grad_rows, preferred_element_type=jnp.float32)
    ffn_grad = reduce_terms(ffn_inner, ffn_outer)
    grad_resid = grad_float + norm_backward(grad_h_two * norm_gains[1], normed_two, scale_two)
    grad_mix = grad_resid.astype(jnp.bfloat16)
    grad_seqs = grad_mix.reshape(seq_count, tok_count, model_width)
    following_hidden, next_grad = shifted((h_seqs[:, :2, :], grad_seqs[:, :2, :]), "ctx", -1)
    grad_ext = jnp.concatenate([grad_seqs, next_grad], axis=1).reshape(
        seq_count * (tok_count + 2), model_width
    )
    c_next = jnp.einsum(
        "qxe,ae->qxa", following_hidden, mixer_backward[:, 1, :], preferred_element_type=jnp.float32
    )
    c_ext = jnp.concatenate([in_c, c_next], axis=1)
    grad_gated = jnp.einsum(
        "rd,cd->rc", grad_ext, mixer_backward[:, 3, :], preferred_element_type=jnp.float32
    )
    grad_gated = grad_gated.reshape(seq_count, tok_count + 2, channel_count)
    grad_mixed = grad_gated * c_ext
    grad_c = grad_gated[:, :tok_count] * mixed_rows
    grad_prod = (
        taps_own[2] * grad_mixed[:, :tok_count]
        + taps_own[1] * grad_mixed[:, 1 : tok_count + 1]
        + taps_own[0] * grad_mixed[:, 2:]
    )
    grad_b = grad_prod * in_x[:, 2:]
    grad_x = grad_prod * in_b[:, 2:]
    gradient_triple = (
        jnp.stack([grad_b, grad_c, grad_x], axis=2)
        .astype(jnp.bfloat16)
        .reshape(row_count, 3, channel_count)
    )
    part_one = jnp.einsum(
        "rkc,ckd->rd", gradient_triple, mixer_backward[:, :3, :], preferred_element_type=jnp.float32
    )
    own_mixed = grad_mixed[:, :tok_count]
    tap_zero = jnp.sum(own_mixed * product[:, :tok_count], axis=(0, 1))
    tap_one = jnp.sum(own_mixed * product[:, 1 : tok_count + 1], axis=(0, 1))
    tap_two = jnp.sum(own_mixed * product[:, 2:], axis=(0, 1))
    tap_grads = jnp.stack([tap_zero, tap_one, tap_two])
    grad_h_one = lax.psum(part_one.astype(jnp.bfloat16), "tp").astype(jnp.float32)
    mixer_inner = jnp.einsum(
        "rkc,rd->ckd", gradient_triple, h_one, preferred_element_type=jnp.float32
    )
    mixer_outer = jnp.einsum(
        "rc,rd->cd", gated_row_block, grad_mix, preferred_element_type=jnp.float32
    )
    mixer_grad = reduce_terms(mixer_inner, mixer_outer)
    gain_terms = jnp.stack(
        [jnp.sum(part_one * normed_one, axis=0), jnp.sum(part_two * normed_two, axis=0)]
    )
    gain_grad, conv_grad = lax.psum(
        (gain_terms, spread_taps(tap_grads, model_width)), ("shard", "ctx", "tp")
    )
    input_grad = grad_resid + norm_backward(grad_h_one * norm_gains[0], normed_one, scale_one)
    input_grad = input_grad.reshape(inputs.shape)
    mixer_new, mixer_first_new, mixer_second_new = adam_update(
        mixer_matrix, mixer_grad, mixer_first, mixer_second, matrix_rate, decay_rate
    )
    ffn_new, ffn_first_new, ffn_second_new = adam_update(
        ffn_weight, ffn_grad, ffn_first, ffn_second, matrix_rate, decay_rate
    )
    conv_new, conv_first_new, conv_second_new = adam_update(
        conv_weight, conv_grad, conv_first, conv_second, small_rate, 0.0
    )
    gain_new, gain_first_new, gain_second_new = adam_update(
        norm_gains, gain_grad, gain_first, gain_second, small_rate, 0.0
    )
    return (
        output,
        input_grad,
        mixer_grad,
        ffn_grad,
        conv_grad,
        gain_grad,
        mixer_new,
        ffn_new,
        conv_new,
        gain_new,
        mixer_first_new,
        mixer_second_new,
        ffn_first_new,
        ffn_second_new,
        conv_first_new,
        conv_second_new,
        gain_first_new,
        gain_second_new,
    )


def solution(mesh):
    in_specs = (
        P("shard", "ctx", None),
        P("shard", "ctx", None),
        P(("shard", "ctx", "tp"), None, None),
        P(("shard", "ctx", "tp"), None, None),
        P(),
        P(),
        P(("shard", "ctx", "tp"), None, None),
        P(("shard", "ctx", "tp"), None, None),
        P(("shard", "ctx", "tp"), None, None),
        P(("shard", "ctx", "tp"), None, None),
        P(),
        P(),
        P(),
        P(),
    )
    out_specs = (
        P("shard", "ctx", None),
        P("shard", "ctx", None),
        P(("shard", "ctx", "tp"), None, None),
        P(("shard", "ctx", "tp"), None, None),
        P(),
        P(),
        P(("shard", "ctx", "tp"), None, None),
        P(("shard", "ctx", "tp"), None, None),
        P(),
        P(),
        P(("shard", "ctx", "tp"), None, None),
        P(("shard", "ctx", "tp"), None, None),
        P(("shard", "ctx", "tp"), None, None),
        P(("shard", "ctx", "tp"), None, None),
        P(),
        P(),
        P(),
        P(),
    )
    return jax.shard_map(
        per_device, mesh=mesh, in_specs=in_specs, out_specs=out_specs, check_vma=False
    )
```

profile of v0, /device:TPU:0, one launch (start us, length us, event | category | flops | bytes accessed | tf_op | source)
XLA Modules:
  0.0 928.6 jit_solution(14838838235188853788)
XLA Ops:
  12.9 5.0 collective-permute-start
  19.2 70.4 %all-gather.3.cloned.1.call-done = bf16[512,4,1024]{2,0,1:T(8,128)(2,1)} async-done(((bf16[32,4,1024]{2,0,1:T(8,128)(2,1)}), bf16[512,4,1024]{2,0,1:T(8,128)(2,1)}) %all-gather.3.cloned.1.call-update) | async-done | bytes 4194320 | tf_op jit(solution)/shard_map/all_gather | solution.py:104
  97.9 16.2 %all-reduce.6.cloned.1.call-done = f32[128,1024]{1,0:T(8,128)} async-done(((f32[128,1024]{1,0:T(8,128)}), f32[128,1024]{1,0:T(8,128)}) %all-reduce.6.cloned.1.call-update) | async-done | bytes 524304 | tf_op jit(solution)/shard_map/psum | solution.py:133
  115.3 169.8 %all-gather.5.cloned.1.call-done = bf16[2304,3,1024]{2,0,1:T(8,128)(2,1)} async-done(((bf16[144,3,1024]{2,0,1:T(8,128)(2,1)}), bf16[2304,3,1024]{2,0,1:T(8,128)(2,1)}) %all-gather.5.cloned.1.call-update) | async-done | bytes 14155792 | tf_op jit(solution)/shard_map/all_gather | solution.py:105
  285.0 6.3 fusion.7
  291.4 5.1 fusion.48
  301.3 16.9 %all-reduce.8.cloned.1.call-done = f32[128,1024]{1,0:T(8,128)} async-done(((f32[128,1024]{1,0:T(8,128)}), f32[128,1024]{1,0:T(8,128)}) %all-reduce.8.cloned.1.call-update) | async-done | bytes 524304 | tf_op jit(solution)/shard_map/psum | solution.py:166
  324.6 7.8 reduce.12
  335.2 6.8 all-to-all-start.1
  343.6 14.7 %collective-permute-done.2 = bf16[1,2,1024]{2,1,0:T(2,128)(2,1)S(1)} collective-permute-done((bf16[1,2,1024]{2,1,0:T(2,128)(2,1)S(1)}, bf16[1,2,1024]{2,1,0:T(2,128)(2,1)S(1)}, u32[]{:S(2)}, u32[]{:S(2)}) %collective-permute-start.2) | collective-permute-done | bytes 4128 | tf_op jit(solution)/shard_map/ppermute | solution.py:19
  361.3 12.7 %collective-permute-done.1 = bf16[1,2,1024]{2,1,0:T(2,128)(2,1)S(1)} collective-permute-done((bf16[1,2,1024]{2,1,0:T(2,128)(2,1)S(1)}, bf16[1,2,1024]{2,1,0:T(2,128)(2,1)S(1)}, u32[]{:S(2)}, u32[]{:S(2)}) %collective-permute-start.1) | collective-permute-done | bytes 4128 | tf_op jit(solution)/shard_map/ppermute | solution.py:19
  379.3 7.8 copy.43
  387.1 5.2 all-to-all-start
  395.7 32.2 %copy.77 = bf16[1,2304,1024]{2,0,1:T(2,128)(2,1)} copy(bf16[1,2304,1024]{2,1,0:T(8,128)(2,1)S(1)} %fusion.4) | data formatting | bytes 9437184 | tf_op jit(solution)/shard_map/convert_element_type | solution.py:71
  427.9 29.0 %reduce.13 = bf16[2304,1024]{1,0:T(8,128)(2,1)} reduce(bf16[2304,1,1024]{2,1,0:T(2,128)(2,1)} %bitcast.200, bf16[]{:T(256)} %broadcast.107), dimensions={1}, to_apply=%bitcast.198.reduce_sub_computation | reduce | bytes 9437186
  456.9 11.8 %reshape.255 = bf16[16,2,73728]{2,1,0:T(2,128)(2,1)} reshape(bf16[2304,1024]{1,0:T(8,128)(2,1)} %reduce.13) | data formatting | bytes 9437184
  468.7 16.8 %all-to-all-done = bf16[1,512,3,1024]{3,2,0,1:T(4,128)(2,1)} async-done(((bf16[1,512,3,1024]{3,2,0,1:T(4,128)(2,1)}), bf16[1,512,3,1024]{3,2,0,1:T(4,128)(2,1)}, u32[]{:S(2)}, u32[]{:S(2)}) %all-to-all-start) | async-done | bytes 3145760 | tf_op jit(solution)/shard_map/all_to_all | solution.py:63
  485.4 4.6 all-to-all-start.3
  490.1 6.3 convert_bitcast_fusion
  496.4 23.9 %copy.47 = bf16[1,2304,2,1024]{3,2,0,1:T(2,128)(2,1)} copy(bf16[1,2304,2,1024]{1,3,2,0:T(8,128)(2,1)} %convert_bitcast_fusion) | data formatting | bytes 18874368 | tf_op jit(solution)/shard_map/convert_element_type | solution.py:64
  520.3 86.0 %all-to-all-done.3 = bf16[16,2,73728]{2,1,0:T(2,128)(2,1)} async-done(((bf16[16,2,73728]{2,1,0:T(2,128)(2,1)}), bf16[16,2,73728]{2,1,0:T(2,128)(2,1)}, u32[]{:S(2)}, u32[]{:S(2)}) %all-to-all-start.3) | async-done | bytes 4718624 | tf_op jit(solution)/shard_map/all_to_all | solution.py:70
  606.2 4.8 all-to-all-start.2
  611.3 4.0 fusion.25
  617.4 19.5 %all-reduce.10.cloned.1.call-done = (bf16[128,1024]{1,0:T(8,128)(2,1)}, bf16[128,1024]{1,0:T(8,128)(2,1)}) async-done(((bf16[128,1024]{1,0:T(8,128)(2,1)}, bf16[128,1024]{1,0:T(8,128)(2,1)}), (bf16[128,1024]{1,0:T(8,128)(2,1)}, bf16[128,1024]{1,0:T(8,128)(2,1)})) %all-reduce.10.cloned.1.call-update) | async-done | bytes 524304 | tf_op jit(solution)/shard_map/psum | solution.py:147
  638.3 216.6 %all-reduce = (f32[3,1024]{1,0:T(4,128)S(1)}, f32[2,1024]{1,0:T(2,128)S(1)}) all-reduce(f32[3,1024]{1,0:T(4,128)S(1)} %reshape.224, f32[2,1024]{1,0:T(2,128)S(1)} %pad_maximum_fusion.9), channel_id=1, replica_groups=mesh['shard'=4,'ctx'=4,'tp'=2] {'shard','ctx','tp'}, use_global_device_ids=true, to_apply=%region_15.16 | all-reduce | flops 5120 | bytes 40960 | tf_op jit(solution)/shard_map/psum | solution.py:218
  863.6 3.4 copy.44
  874.2 13.1 %reshape.256 = bf16[2304,1,1024]{2,1,0:T(2,128)(2,1)} reshape(bf16[16,2,73728]{2,1,0:T(2,128)(2,1)} %all-to-all-done.3) | data formatting | bytes 9437184
  887.2 9.6 %copy.63 = f32[1,2304,1024]{2,1,0:T(8,128)} copy(bf16[1,2304,1024]{2,0,1:T(2,128)(2,1)} %bitcast.202) | data formatting | bytes 14155776
  896.8 4.7 reduce_sum.124
  901.5 10.4 %copy.48 = bf16[1,2304,2,1024]{3,1,2,0:T(8,128)(2,1)} copy(bf16[1,2304,2,1024]{3,2,0,1:T(2,128)(2,1)} %all-to-all-done.2) | data formatting | bytes 18874368 | tf_op jit(solution)/shard_map/all_to_all | solution.py:63
  911.9 6.3 convert_reduce_fusion
  918.3 3.5 multiply_subtract_fusion
  (168 shorter events, 62.9 us)
Async XLA Ops:
  7.2 82.4 %all-gather.3.cloned.1.call-start = ((), (), s32[]{:S(2)}) async-start(), calls=%async_computation.4 | async-start | bytes 4456448 | tf_op jit(solution)/shard_map/all_gather | solution.py:104
  9.3 104.8 %all-reduce.6.cloned.1.call-start = ((), (), s32[]{:S(2)}) async-start(), calls=%async_computation.5 | async-start | bytes 1048576 | tf_op jit(solution)/shard_map/psum | solution.py:133
  11.3 309.1 %copy-start.23 = (f32[1,1024]{1,0:T(1,128)}, f32[1,1024]{1,0:T(1,128)S(1)}, u32[]{:S(2)}) copy-start(f32[1,1024]{1,0:T(1,128)S(1)} %get-tuple-element.80) | copy-start | bytes 12292
  12.9 6.3 collective-permute-start
  18.2 74.5 %copy-start.28 = (f32[512]{0:T(512)}, f32[512]{0:T(512)S(1)}, u32[]{:S(2)}) copy-start(f32[512]{0:T(512)S(1)} %mul.367) | copy-start | bytes 6148
  18.3 74.4 %copy-start.30 = (f32[512]{0:T(512)}, f32[512]{0:T(512)S(1)}, u32[]{:S(2)}) copy-start(f32[512]{0:T(512)S(1)} %mul.371) | copy-start | bytes 6148
  18.4 74.4 %copy-start.32 = (f32[512]{0:T(512)}, f32[512]{0:T(512)S(1)}, u32[]{:S(2)}) copy-start(f32[512]{0:T(512)S(1)} %mul.374) | copy-start | bytes 6148
  96.7 17.4 %copy-start = (bf16[1,128,1024]{2,1,0:T(8,128)(2,1)S(1)}, bf16[1,128,1024]{2,1,0:T(8,128)(2,1)}, u32[]{:S(2)}) copy-start(bf16[1,128,1024]{2,1,0:T(8,128)(2,1)} %param.14) | copy-start | bytes 786436
  96.7 188.3 %all-gather.5.cloned.1.call-start = ((), (), s32[]{:S(2)}) async-start(), calls=%async_computation.6 | async-start | bytes 15040512 | tf_op jit(solution)/shard_map/all_gather | solution.py:105
  97.9 220.4 %all-reduce.8.cloned.1.call-start = ((), (), s32[]{:S(2)}) async-start(), calls=%async_computation.7 | async-start | bytes 1048576 | tf_op jit(solution)/shard_map/psum | solution.py:166
  115.3 205.1 %copy-start.43 = (f32[128]{0:T(128)}, f32[128]{0:T(128)S(1)}, u32[]{:S(2)}) copy-start(f32[128]{0:T(128)S(1)} %add_rsqrt_fusion) | copy-start | bytes 1540
  335.2 51.9 %all-to-all-start.1 = ((bf16[16,2,16384]{2,1,0:T(2,128)(2,1)}), bf16[16,2,16384]{2,1,0:T(2,128)(2,1)S(1)}, u32[]{:S(2)}, u32[]{:S(2)}) async-start(bf16[16,2,16384]{2,1,0:T(2,128)(2,1)} %reshape.253), calls=%async_computation.1 | async-start | bytes 2097152 | tf_op jit(solution)/shard_map/all_to_all | solution.py:70
  342.1 17.8 %copy-start.20 = (bf16[1,128,1024]{2,1,0:T(8,128)(2,1)S(1)}, bf16[1,128,1024]{2,1,0:T(8,128)(2,1)}, u32[]{:S(2)}) copy-start(bf16[1,128,1024]{2,1,0:T(8,128)(2,1)} %get-tuple-element.65) | copy-start | bytes 786436
  342.1 16.2 %collective-permute-start.2 = (bf16[1,2,1024]{2,1,0:T(2,128)(2,1)S(1)}, bf16[1,2,1024]{2,1,0:T(2,128)(2,1)S(1)}, u32[]{:S(2)}, u32[]{:S(2)}) collective-permute-start(bf16[1,2,1024]{2,1,0:T(2,128)(2,1)S(1)} %get-tuple-element.78), channel_id=1, source_target_pairs={{2,0},{4,2},{6,4},{3,1},{5,3},{7,5},{10,8},{12,10},{14,12},{11,9},... | collective-permute-start | bytes 12296 | tf_op jit(solution)/shard_map/ppermute | solution.py:19
  359.8 16.0 %copy-start.31 = (f32[512]{0:T(512)S(1)}, f32[512]{0:T(512)}, u32[]{:S(2)}) copy-start(f32[512]{0:T(512)} %copy-done.30) | copy-start | bytes 6148
  359.8 16.0 %copy-start.33 = (f32[512]{0:T(512)S(1)}, f32[512]{0:T(512)}, u32[]{:S(2)}) copy-start(f32[512]{0:T(512)} %copy-done.32) | copy-start | bytes 6148
  359.9 14.2 %collective-permute-start.1 = (bf16[1,2,1024]{2,1,0:T(2,128)(2,1)S(1)}, bf16[1,2,1024]{2,1,0:T(2,128)(2,1)S(1)}, u32[]{:S(2)}, u32[]{:S(2)}) collective-permute-start(bf16[1,2,1024]{2,1,0:T(2,128)(2,1)S(1)} %slice.137), channel_id=1, source_target_pairs={{2,0},{4,2},{6,4},{3,1},{5,3},{7,5},{10,8},{12,10},{14,12},{11,9},... | collective-permute-start | bytes 12296 | tf_op jit(solution)/shard_map/ppermute | solution.py:19
  387.1 98.4 %all-to-all-start = ((bf16[1,512,3,1024]{3,2,0,1:T(4,128)(2,1)}), bf16[1,512,3,1024]{3,2,0,1:T(4,128)(2,1)}, u32[]{:S(2)}, u32[]{:S(2)}) async-start(bf16[1,512,3,1024]{3,2,0,1:T(4,128)(2,1)} %copy.43), calls=%async_computation | async-start | bytes 8388608 | tf_op jit(solution)/shard_map/all_to_all | solution.py:63
  468.6 21.4 %copy-start.24 = (f32[1,1024]{1,0:T(1,128)S(1)}, f32[1,1024]{1,0:T(1,128)}, u32[]{:S(2)}) copy-start(f32[1,1024]{1,0:T(1,128)} %copy-done.23) | copy-start | bytes 12292
  468.6 21.4 %copy-start.44 = (f32[128]{0:T(128)S(1)}, f32[128]{0:T(128)}, u32[]{:S(2)}) copy-start(f32[128]{0:T(128)} %copy-done.43) | copy-start | bytes 1540
  485.4 120.8 %all-to-all-start.3 = ((bf16[16,2,73728]{2,1,0:T(2,128)(2,1)}), bf16[16,2,73728]{2,1,0:T(2,128)(2,1)}, u32[]{:S(2)}, u32[]{:S(2)}) async-start(bf16[16,2,73728]{2,1,0:T(2,128)(2,1)} %reshape.255), calls=%async_computation.3 | async-start | bytes 9437184 | tf_op jit(solution)/shard_map/all_to_all | solution.py:70
  606.2 295.3 %all-to-all-start.2 = ((bf16[1,2304,2,1024]{3,2,0,1:T(2,128)(2,1)}), bf16[1,2304,2,1024]{3,2,0,1:T(2,128)(2,1)}, u32[]{:S(2)}, u32[]{:S(2)}) async-start(bf16[1,2304,2,1024]{3,2,0,1:T(2,128)(2,1)} %copy.47), calls=%async_computation.2 | async-start | bytes 18874368 | tf_op jit(solution)/shard_map/all_to_all | solution.py:63
  611.0 25.8 %all-reduce.10.cloned.1.call-start = ((), (), s32[]{:S(2)}) async-start(), calls=%async_computation.8 | async-start | bytes 1048576 | tf_op jit(solution)/shard_map/psum | solution.py:147
  616.8 21.5 %copy-start.34 = (f32[1024]{0:T(1024)S(1)}, f32[1024]{0:T(1024)}, u32[]{:S(2)}) copy-start(f32[1024]{0:T(1024)} %get-tuple-element.39) | copy-start | bytes 12292
  616.8 238.2 %copy-start.27 = (f32[2,1024]{1,0:T(2,128)S(1)}, f32[2,1024]{1,0:T(2,128)}, u32[]{:S(2)}) copy-start(f32[2,1024]{1,0:T(2,128)} %param.19) | copy-start | bytes 24580
  616.8 238.2 %copy-start.40 = (f32[2,1024]{1,0:T(2,128)S(1)}, f32[2,1024]{1,0:T(2,128)}, u32[]{:S(2)}) copy-start(f32[2,1024]{1,0:T(2,128)} %param.26) | copy-start | bytes 24580
  616.8 238.2 %copy-start.41 = (f32[2,1024]{1,0:T(2,128)S(1)}, f32[2,1024]{1,0:T(2,128)}, u32[]{:S(2)}) copy-start(f32[2,1024]{1,0:T(2,128)} %param.27) | copy-start | bytes 24580
  616.8 238.9 %copy-start.26 = (f32[3,1024]{1,0:T(4,128)S(1)}, f32[3,1024]{1,0:T(4,128)}, u32[]{:S(2)}) copy-start(f32[3,1024]{1,0:T(4,128)} %param.18) | copy-start | bytes 36868
  616.8 238.9 %copy-start.35 = (f32[3,1024]{1,0:T(4,128)S(1)}, f32[3,1024]{1,0:T(4,128)}, u32[]{:S(2)}) copy-start(f32[3,1024]{1,0:T(4,128)} %param.24) | copy-start | bytes 36868
  616.8 238.9 %copy-start.36 = (f32[3,1024]{1,0:T(4,128)S(1)}, f32[3,1024]{1,0:T(4,128)}, u32[]{:S(2)}) copy-start(f32[3,1024]{1,0:T(4,128)} %param.25) | copy-start | bytes 36868
  616.8 241.2 %copy-start.4 = (f32[128,1024]{1,0:T(8,128)S(1)}, f32[128,1024]{1,0:T(8,128)}, u32[]{:S(2)}) copy-start(f32[128,1024]{1,0:T(8,128)} %copy-done.3) | copy-start | bytes 1572868
  636.9 221.2 %copy-start.12 = (bf16[128,1024]{1,0:T(8,128)(2,1)S(1)}, bf16[128,1024]{1,0:T(8,128)(2,1)}, u32[]{:S(2)}) copy-start(bf16[128,1024]{1,0:T(8,128)(2,1)} %get-tuple-element.49) | copy-start | bytes 786436
  (26 other events, 136.0 us)
Sparse Core Ops, SparseCore 0:
  11.4 78.1 all-gather.2
  96.8 17.1 all-reduce.5
  117.5 167.4 all-gather.4
  301.4 16.7 all-reduce.7
  617.0 19.8 all-reduce.9
where the time goes:
time: 934 us; the launch traced here: 929 us
  waiting for transfers between devices  424 us (45%)
  blocking collectives  217 us (23%)
  local copies, waits for them, and re-layouts  134 us (14%)
  other arithmetic  70.8 us (8%)
  matrix products  38.6 us (4%)
  starting transfers between devices  29.7 us (3%)
  between operations  14.8 us (2%)
    psum x1, blocking collectives, per_device(): lax.psum((gain_terms, spread_taps(tap_grads, model_width)), ('shard', 'ct...  217 us
    all_gather x1, waiting for transfers between devices, per_device(): lax.all_gather(ffn_half, ('shard', 'ctx'), axis=0, tiled=True)  170 us
    all_to_all x2, waiting for transfers between devices, reduce_terms(): lax.all_to_all(outer_term[None].astype(jnp.bfloat16), ('shard', 'ctx'), s...  86 us
    all_gather x1, waiting for transfers between devices, per_device(): lax.all_gather(mixer_half, ('shard', 'ctx'), axis=0, tiled=True)  70.4 us
    unnamed x104, local copies, waits for them, and re-layouts  53.3 us
    unnamed x2, other arithmetic  36.7 us
    convert_element_type x2, local copies, waits for them, and re-layouts, reduce_terms(): outer_term[None].astype(jnp.bfloat16)  33.8 us
    convert_element_type x2, local copies, waits for them, and re-layouts, reduce_terms(): inner_term[None].astype(jnp.bfloat16)  31.7 us
  transfers between devices with their start and end apart: 12, of which 10 were waited for; matrix products, arithmetic and copies ran while one was open for 19% of the time, Pallas kernels for 0%

commit v1 on v0

--- a/solution.py
+++ b/solution.py
@@ -11,6 +11,16 @@
 matrix_rate = 0.02
 small_rate = 0.25
 decay_rate = 0.1
+
+
+def ring_gather(x, axis, dim):
+    ways, here, step = (lax.axis_size(axis), lax.axis_index(axis), x.shape[dim])
+    dims = [n * ways if d == dim else n for d, n in enumerate(x.shape)]
+    full = lax.dynamic_update_slice_in_dim(jnp.zeros(dims, x.dtype), x, here * step, axis=dim)
+    for far in range(1, ways):
+        x = lax.ppermute(x, axis, [(d, (d + 1) % ways) for d in range(ways)])
+        full = lax.dynamic_update_slice_in_dim(full, x, (here - far) % ways * step, axis=dim)
+    return full
 
 
 def shifted(value, axis, steps):
@@ -102,7 +112,7 @@
     ffn_half = ffn_weight.astype(jnp.bfloat16)
     mixer_whole, ffn_whole = (
         lax.all_gather(mixer_half, ("shard", "ctx"), axis=0, tiled=True),
-        lax.all_gather(ffn_half, ("shard", "ctx"), axis=0, tiled=True),
+        ring_gather(ffn_half, ("shard", "ctx"), 0),
     )
     channel_count = mixer_whole.shape[0]
     x_rows = inputs.reshape(row_count, model_width).astype(jnp.float32)

time: 934 us -> 1200 us (1.28)
  waiting for transfers between devices: 424 us -> 644 us
  local copies, waits for them, and re-layouts: 134 us -> 170 us
  starting transfers between devices: 29.7 us -> 42.5 us
    ppermute x0 -> x15, waiting for transfers between devices: none -> 432 us  [ring_gather(): x = lax.ppermute(x, axis, [(d, (d + 1) % ways) for d in range(ways)])]
    all_gather x1, waiting for transfers between devices: 170 us -> 0.02 us  [per_device(): lax.all_gather(ffn_half, ('shard', 'ctx'), axis=0, tiled=True)]
    all_to_all x2, waiting for transfers between devices: 86 us -> 40.9 us  [reduce_terms(): lax.all_to_all(outer_term[None].astype(jnp.bfloat16), ('shard', 'ctx'), s...]
    all_to_all x2, waiting for transfers between devices: 16.8 us -> 61.2 us  [reduce_terms(): lax.all_to_all(inner_term[None].astype(jnp.bfloat16), ('shard', 'ctx'), s...]
    dynamic_update_slice x0 -> x15, local copies, waits for them, and re-layouts: none -> 19.8 us  [ring_gather(): lax.dynamic_update_slice_in_dim(full, x, (here - far) % ways * step, axis...]
    psum x1, waiting for transfers between devices: 19.5 us -> 0.02 us  [per_device(): ffn_out = lax.psum(ffn_part.astype(jnp.bfloat16), 'tp').astype(jnp.float32)]
    psum x1, waiting for transfers between devices: 16.2 us -> 0.01 us  [per_device(): mix_out = lax.psum(mix_part, 'tp')]
    ppermute x0 -> x15, starting transfers between devices: none -> 15.2 us  [ring_gather(): x = lax.ppermute(x, axis, [(d, (d + 1) % ways) for d in range(ways)])]
  transfers between devices with their start and end apart: 12 -> 27, of which waited for: 10 -> 22; matrix products, arithmetic and copies ran while one was open for 19% -> 20% of each run, Pallas kernels for 0% -> 0%
where the time goes in v1:
time: 1200 us; the launch traced here: 1190 us
  waiting for transfers between devices  644 us (54%)
  blocking collectives  212 us (18%)
  local copies, waits for them, and re-layouts  170 us (14%)
  other arithmetic  70.7 us (6%)
  starting transfers between devices  42.5 us (4%)
  matrix products  36.9 us (3%)
  between operations  15.2 us (1%)
    ppermute x15, waiting for transfers between devices, ring_gather(): x = lax.ppermute(x, axis, [(d, (d + 1) % ways) for d in range(ways)])  432 us
    psum x1, blocking collectives, per_device(): lax.psum((gain_terms, spread_taps(tap_grads, model_width)), ('shard', 'ct...  212 us
    all_gather x1, waiting for transfers between devices, per_device(): lax.all_gather(mixer_half, ('shard', 'ctx'), axis=0, tiled=True)  69.8 us
    all_to_all x2, waiting for transfers between devices, reduce_terms(): lax.all_to_all(inner_term[None].astype(jnp.bfloat16), ('shard', 'ctx'), s...  61.2 us
    unnamed x148, local copies, waits for them, and re-layouts  58.5 us
    all_to_all x2, waiting for transfers between devices, reduce_terms(): lax.all_to_all(outer_term[None].astype(jnp.bfloat16), ('shard', 'ctx'), s...  40.9 us
    unnamed x2, other arithmetic  36.7 us
    convert_element_type x2, local copies, waits for them, and re-layouts, reduce_terms(): outer_term[None].astype(jnp.bfloat16)  33.8 us
  transfers between devices with their start and end apart: 27, of which 22 were waited for; matrix products, arithmetic and copies ran while one was open for 20% of the time, Pallas kernels for 0%

profile of v1, /device:TPU:0, one launch (start us, length us, event | category | flops | bytes accessed | tf_op | source)
XLA Modules:
  0.0 1191.4 jit_solution(13247738175634158952)
XLA Ops:
  19.8 69.8 %all-gather.3.cloned.1.call-done = bf16[512,4,1024]{2,0,1:T(8,128)(2,1)} async-done(((bf16[32,4,1024]{2,0,1:T(8,128)(2,1)}), bf16[512,4,1024]{2,0,1:T(8,128)(2,1)}) %all-gather.3.cloned.1.call-update) | async-done | bytes 4194320 | tf_op jit(solution)/shard_map/all_gather | solution.py:114
  96.8 6.9 broadcast_in_dim.9
  106.7 22.1 %collective-permute-done.1 = bf16[144,3,1024]{2,0,1:T(8,128)(2,1)S(1)} collective-permute-done((bf16[144,3,1024]{2,0,1:T(8,128)(2,1)}, bf16[144,3,1024]{2,0,1:T(8,128)(2,1)S(1)}, u32[]{:S(2)}, u32[]{:S(2)}) %collective-permute-start.1) | collective-permute-done | bytes 884768 | tf_op jit(solution)/shard_map/ppermute | solution.py:21
  128.8 42.0 %collective-permute-done.2 = bf16[144,3,1024]{2,0,1:T(8,128)(2,1)S(1)} collective-permute-done((bf16[144,3,1024]{2,0,1:T(8,128)(2,1)S(1)}, bf16[144,3,1024]{2,0,1:T(8,128)(2,1)S(1)}, u32[]{:S(2)}, u32[]{:S(2)}) %collective-permute-start.2) | collective-permute-done | bytes 884768 | tf_op jit(solution)/shard_map/ppermute | solution.py:21
  170.8 42.9 %collective-permute-done.3 = bf16[144,3,1024]{2,0,1:T(8,128)(2,1)S(1)} collective-permute-done((bf16[144,3,1024]{2,0,1:T(8,128)(2,1)S(1)}, bf16[144,3,1024]{2,0,1:T(8,128)(2,1)S(1)}, u32[]{:S(2)}, u32[]{:S(2)}) %collective-permute-start.3) | collective-permute-done | bytes 884768 | tf_op jit(solution)/shard_map/ppermute | solution.py:21
  214.6 35.8 %collective-permute-done.4 = bf16[144,3,1024]{2,0,1:T(8,128)(2,1)S(1)} collective-permute-done((bf16[144,3,1024]{2,0,1:T(8,128)(2,1)S(1)}, bf16[144,3,1024]{2,0,1:T(8,128)(2,1)S(1)}, u32[]{:S(2)}, u32[]{:S(2)}) %collective-permute-start.4) | collective-permute-done | bytes 884768 | tf_op jit(solution)/shard_map/ppermute | solution.py:21
  251.3 42.5 %collective-permute-done.5 = bf16[144,3,1024]{2,0,1:T(8,128)(2,1)S(1)} collective-permute-done((bf16[144,3,1024]{2,0,1:T(8,128)(2,1)S(1)}, bf16[144,3,1024]{2,0,1:T(8,128)(2,1)S(1)}, u32[]{:S(2)}, u32[]{:S(2)}) %collective-permute-start.5) | collective-permute-done | bytes 884768 | tf_op jit(solution)/shard_map/ppermute | solution.py:21
  293.9 39.3 %collective-permute-done.6 = bf16[144,3,1024]{2,0,1:T(8,128)(2,1)S(1)} collective-permute-done((bf16[144,3,1024]{2,0,1:T(8,128)(2,1)S(1)}, bf16[144,3,1024]{2,0,1:T(8,128)(2,1)S(1)}, u32[]{:S(2)}, u32[]{:S(2)}) %collective-permute-start.6) | collective-permute-done | bytes 884768 | tf_op jit(solution)/shard_map/ppermute | solution.py:21
  333.1 13.4 %collective-permute-start.7 = (bf16[144,3,1024]{2,0,1:T(8,128)(2,1)S(1)}, bf16[144,3,1024]{2,0,1:T(8,128)(2,1)S(1)}, u32[]{:S(2)}, u32[]{:S(2)}) collective-permute-start(bf16[144,3,1024]{2,0,1:T(8,128)(2,1)S(1)} %collective-permute-done.6), channel_id=1, source_target_pairs={{0,2},{2,4},{4,6},{6,8},{8,10},{10,12},{12,14},{14,16},{16,18},{18... | collective-permute-start | bytes 2654216 | tf_op jit(solution)/shard_map/ppermute | solution.py:21
  346.5 39.7 %collective-permute-done.7 = bf16[144,3,1024]{2,0,1:T(8,128)(2,1)S(1)} collective-permute-done((bf16[144,3,1024]{2,0,1:T(8,128)(2,1)S(1)}, bf16[144,3,1024]{2,0,1:T(8,128)(2,1)S(1)}, u32[]{:S(2)}, u32[]{:S(2)}) %collective-permute-start.7) | collective-permute-done | bytes 884768 | tf_op jit(solution)/shard_map/ppermute | solution.py:21
  386.2 24.9 %collective-permute-done.8 = bf16[144,3,1024]{2,0,1:T(8,128)(2,1)S(1)} collective-permute-done((bf16[144,3,1024]{2,0,1:T(8,128)(2,1)S(1)}, bf16[144,3,1024]{2,0,1:T(8,128)(2,1)S(1)}, u32[]{:S(2)}, u32[]{:S(2)}) %collective-permute-start.8) | collective-permute-done | bytes 884768 | tf_op jit(solution)/shard_map/ppermute | solution.py:21
  411.1 26.1 %collective-permute-done.9 = bf16[144,3,1024]{2,0,1:T(8,128)(2,1)S(1)} collective-permute-done((bf16[144,3,1024]{2,0,1:T(8,128)(2,1)S(1)}, bf16[144,3,1024]{2,0,1:T(8,128)(2,1)S(1)}, u32[]{:S(2)}, u32[]{:S(2)}) %collective-permute-start.9) | collective-permute-done | bytes 884768 | tf_op jit(solution)/shard_map/ppermute | solution.py:21
  437.2 25.3 %collective-permute-done.10 = bf16[144,3,1024]{2,0,1:T(8,128)(2,1)S(1)} collective-permute-done((bf16[144,3,1024]{2,0,1:T(8,128)(2,1)S(1)}, bf16[144,3,1024]{2,0,1:T(8,128)(2,1)S(1)}, u32[]{:S(2)}, u32[]{:S(2)}) %collective-permute-start.10) | collective-permute-done | bytes 884768 | tf_op jit(solution)/shard_map/ppermute | solution.py:21
  462.5 25.3 %collective-permute-done.11 = bf16[144,3,1024]{2,0,1:T(8,128)(2,1)S(1)} collective-permute-done((bf16[144,3,1024]{2,0,1:T(8,128)(2,1)S(1)}, bf16[144,3,1024]{2,0,1:T(8,128)(2,1)S(1)}, u32[]{:S(2)}, u32[]{:S(2)}) %collective-permute-start.11) | collective-permute-done | bytes 884768 | tf_op jit(solution)/shard_map/ppermute | solution.py:21
  488.8 23.9 %collective-permute-done.12 = bf16[144,3,1024]{2,0,1:T(8,128)(2,1)} collective-permute-done((bf16[144,3,1024]{2,0,1:T(8,128)(2,1)S(1)}, bf16[144,3,1024]{2,0,1:T(8,128)(2,1)}, u32[]{:S(2)}, u32[]{:S(2)}) %collective-permute-start.12) | collective-permute-done | bytes 884768 | tf_op jit(solution)/shard_map/ppermute | solution.py:21
  518.4 17.5 %collective-permute-done.13 = bf16[144,3,1024]{2,0,1:T(8,128)(2,1)} collective-permute-done((bf16[144,3,1024]{2,0,1:T(8,128)(2,1)}, bf16[144,3,1024]{2,0,1:T(8,128)(2,1)}, u32[]{:S(2)}, u32[]{:S(2)}) %collective-permute-start.13) | collective-permute-done | bytes 884768 | tf_op jit(solution)/shard_map/ppermute | solution.py:21
  542.1 16.3 %collective-permute-done.14 = bf16[144,3,1024]{2,0,1:T(8,128)(2,1)} collective-permute-done((bf16[144,3,1024]{2,0,1:T(8,128)(2,1)}, bf16[144,3,1024]{2,0,1:T(8,128)(2,1)}, u32[]{:S(2)}, u32[]{:S(2)}) %collective-permute-start.14) | collective-permute-done | bytes 884768 | tf_op jit(solution)/shard_map/ppermute | solution.py:21
  567.2 8.3 collective-permute-done.15
  584.4 32.2 %copy.92 = bf16[1,2304,1024]{2,0,1:T(2,128)(2,1)} copy(bf16[1,2304,1024]{2,1,0:T(8,128)(2,1)S(1)} %fusion.2) | data formatting | bytes 9437184 | tf_op jit(solution)/shard_map/convert_element_type | solution.py:81
  617.1 28.9 %reduce.13 = bf16[2304,1024]{1,0:T(8,128)(2,1)} reduce(bf16[2304,1,1024]{2,1,0:T(2,128)(2,1)} %bitcast.203, bf16[]{:T(256)} %broadcast.122), dimensions={1}, to_apply=%bitcast.201.reduce_sub_computation | reduce | bytes 9437186
  646.0 11.8 reshape.255
  672.7 20.0 %all-reduce.8.cloned.1.call-done = f32[128,1024]{1,0:T(8,128)} async-done(((f32[128,1024]{1,0:T(8,128)}), f32[128,1024]{1,0:T(8,128)}) %all-reduce.8.cloned.1.call-update) | async-done | bytes 524304 | tf_op jit(solution)/shard_map/psum | solution.py:176
  698.9 7.8 reduce.12
  709.7 40.9 %all-to-all-done.3 = bf16[16,2,73728]{2,1,0:T(2,128)(2,1)} async-done(((bf16[16,2,73728]{2,1,0:T(2,128)(2,1)}), bf16[16,2,73728]{2,1,0:T(2,128)(2,1)}, u32[]{:S(2)}, u32[]{:S(2)}) %all-to-all-start.3) | async-done | bytes 4718624 | tf_op jit(solution)/shard_map/all_to_all | solution.py:80
  767.0 13.8 %collective-permute-done.16 = bf16[1,2,1024]{2,1,0:T(2,128)(2,1)S(1)} collective-permute-done((bf16[1,2,1024]{2,1,0:T(2,128)(2,1)S(1)}, bf16[1,2,1024]{2,1,0:T(2,128)(2,1)S(1)}, u32[]{:S(2)}, u32[]{:S(2)}) %collective-permute-start.16) | collective-permute-done | bytes 4128 | tf_op jit(solution)/shard_map/ppermute | solution.py:29
  787.1 7.8 copy.54
  806.9 24.0 %copy.59 = bf16[1,2304,2,1024]{3,2,0,1:T(2,128)(2,1)} copy(bf16[1,2304,2,1024]{1,3,2,0:T(8,128)(2,1)} %convert_bitcast_fusion) | data formatting | bytes 18874368 | tf_op jit(solution)/shard_map/convert_element_type | solution.py:74
  830.8 61.2 %all-to-all-done = bf16[1,512,3,1024]{3,2,0,1:T(4,128)(2,1)} async-done(((bf16[1,512,3,1024]{3,2,0,1:T(4,128)(2,1)}), bf16[1,512,3,1024]{3,2,0,1:T(4,128)(2,1)}, u32[]{:S(2)}, u32[]{:S(2)}) %all-to-all-start) | async-done | bytes 3145760 | tf_op jit(solution)/shard_map/all_to_all | solution.py:73
  902.4 12.9 %reshape.256 = bf16[2304,1,1024]{2,1,0:T(2,128)(2,1)} reshape(bf16[16,2,73728]{2,1,0:T(2,128)(2,1)} %all-to-all-done.3) | data formatting | bytes 9437184
  915.4 9.7 copy.78
  932.0 211.7 %all-reduce = (f32[3,1024]{1,0:T(4,128)S(1)}, f32[2,1024]{1,0:T(2,128)S(1)}) all-reduce(f32[3,1024]{1,0:T(4,128)S(1)} %reshape.224, f32[2,1024]{1,0:T(2,128)S(1)} %pad_maximum_fusion.9), channel_id=1, replica_groups=mesh['shard'=4,'ctx'=4,'tp'=2] {'shard','ctx','tp'}, use_global_device_ids=true, to_apply=%region_15.16 | all-reduce | flops 5120 | bytes 40960 | tf_op jit(solution)/shard_map/psum | solution.py:228
  1164.5 10.4 copy.60
  (258 shorter events, 161.4 us)
Async XLA Ops:
  7.2 82.4 %all-gather.3.cloned.1.call-start = ((), (), s32[]{:S(2)}) async-start(), calls=%async_computation.4 | async-start | bytes 4456448 | tf_op jit(solution)/shard_map/all_gather | solution.py:114
  9.3 531.6 %all-reduce.6.cloned.1.call-start = ((), (), s32[]{:S(2)}) async-start(), calls=%async_computation.5 | async-start | bytes 1048576 | tf_op jit(solution)/shard_map/psum | solution.py:143
  13.5 6.3 collective-permute-start
  96.7 566.8 %all-gather.5.cloned.1.call-start = ((), (), s32[]{:S(2)}) async-start(), calls=%async_computation.6 | async-start | bytes 15040512 | tf_op jit(solution)/shard_map/all_gather | solution.py:161
  105.2 23.7 %collective-permute-start.1 = (bf16[144,3,1024]{2,0,1:T(8,128)(2,1)}, bf16[144,3,1024]{2,0,1:T(8,128)(2,1)S(1)}, u32[]{:S(2)}, u32[]{:S(2)}) collective-permute-start(bf16[144,3,1024]{2,0,1:T(8,128)(2,1)} %get-tuple-element.70), channel_id=1, source_target_pairs={{0,2},{2,4},{4,6},{6,8},{8,10},{10,12},{12,14},{14,16},{16,18},{18... | collective-permute-start | bytes 2654216 | tf_op jit(solution)/shard_map/ppermute | solution.py:21
  128.8 42.0 %collective-permute-start.2 = (bf16[144,3,1024]{2,0,1:T(8,128)(2,1)S(1)}, bf16[144,3,1024]{2,0,1:T(8,128)(2,1)S(1)}, u32[]{:S(2)}, u32[]{:S(2)}) collective-permute-start(bf16[144,3,1024]{2,0,1:T(8,128)(2,1)S(1)} %collective-permute-done.1), channel_id=1, source_target_pairs={{0,2},{2,4},{4,6},{6,8},{8,10},{10,12},{12,14},{14,16},{16,18},{18... | collective-permute-start | bytes 2654216 | tf_op jit(solution)/shard_map/ppermute | solution.py:21
  170.8 42.9 %collective-permute-start.3 = (bf16[144,3,1024]{2,0,1:T(8,128)(2,1)S(1)}, bf16[144,3,1024]{2,0,1:T(8,128)(2,1)S(1)}, u32[]{:S(2)}, u32[]{:S(2)}) collective-permute-start(bf16[144,3,1024]{2,0,1:T(8,128)(2,1)S(1)} %collective-permute-done.2), channel_id=1, source_target_pairs={{0,2},{2,4},{4,6},{6,8},{8,10},{10,12},{12,14},{14,16},{16,18},{18... | collective-permute-start | bytes 2654216 | tf_op jit(solution)/shard_map/ppermute | solution.py:21
  213.7 36.8 %collective-permute-start.4 = (bf16[144,3,1024]{2,0,1:T(8,128)(2,1)S(1)}, bf16[144,3,1024]{2,0,1:T(8,128)(2,1)S(1)}, u32[]{:S(2)}, u32[]{:S(2)}) collective-permute-start(bf16[144,3,1024]{2,0,1:T(8,128)(2,1)S(1)} %collective-permute-done.3), channel_id=1, source_target_pairs={{0,2},{2,4},{4,6},{6,8},{8,10},{10,12},{12,14},{14,16},{16,18},{18... | collective-permute-start | bytes 2654216 | tf_op jit(solution)/shard_map/ppermute | solution.py:21
  250.4 43.4 %collective-permute-start.5 = (bf16[144,3,1024]{2,0,1:T(8,128)(2,1)S(1)}, bf16[144,3,1024]{2,0,1:T(8,128)(2,1)S(1)}, u32[]{:S(2)}, u32[]{:S(2)}) collective-permute-start(bf16[144,3,1024]{2,0,1:T(8,128)(2,1)S(1)} %collective-permute-done.4), channel_id=1, source_target_pairs={{0,2},{2,4},{4,6},{6,8},{8,10},{10,12},{12,14},{14,16},{16,18},{18... | collective-permute-start | bytes 2654216 | tf_op jit(solution)/shard_map/ppermute | solution.py:21
  293.9 39.3 %collective-permute-start.6 = (bf16[144,3,1024]{2,0,1:T(8,128)(2,1)S(1)}, bf16[144,3,1024]{2,0,1:T(8,128)(2,1)S(1)}, u32[]{:S(2)}, u32[]{:S(2)}) collective-permute-start(bf16[144,3,1024]{2,0,1:T(8,128)(2,1)S(1)} %collective-permute-done.5), channel_id=1, source_target_pairs={{0,2},{2,4},{4,6},{6,8},{8,10},{10,12},{12,14},{14,16},{16,18},{18... | collective-permute-start | bytes 2654216 | tf_op jit(solution)/shard_map/ppermute | solution.py:21
  333.1 53.1 %collective-permute-start.7 = (bf16[144,3,1024]{2,0,1:T(8,128)(2,1)S(1)}, bf16[144,3,1024]{2,0,1:T(8,128)(2,1)S(1)}, u32[]{:S(2)}, u32[]{:S(2)}) collective-permute-start(bf16[144,3,1024]{2,0,1:T(8,128)(2,1)S(1)} %collective-permute-done.6), channel_id=1, source_target_pairs={{0,2},{2,4},{4,6},{6,8},{8,10},{10,12},{12,14},{14,16},{16,18},{18... | collective-permute-start | bytes 2654216 | tf_op jit(solution)/shard_map/ppermute | solution.py:21
  386.2 24.9 %collective-permute-start.8 = (bf16[144,3,1024]{2,0,1:T(8,128)(2,1)S(1)}, bf16[144,3,1024]{2,0,1:T(8,128)(2,1)S(1)}, u32[]{:S(2)}, u32[]{:S(2)}) collective-permute-start(bf16[144,3,1024]{2,0,1:T(8,128)(2,1)S(1)} %collective-permute-done.7), channel_id=1, source_target_pairs={{0,2},{2,4},{4,6},{6,8},{8,10},{10,12},{12,14},{14,16},{16,18},{18... | collective-permute-start | bytes 2654216 | tf_op jit(solution)/shard_map/ppermute | solution.py:21
  411.1 26.1 %collective-permute-start.9 = (bf16[144,3,1024]{2,0,1:T(8,128)(2,1)S(1)}, bf16[144,3,1024]{2,0,1:T(8,128)(2,1)S(1)}, u32[]{:S(2)}, u32[]{:S(2)}) collective-permute-start(bf16[144,3,1024]{2,0,1:T(8,128)(2,1)S(1)} %collective-permute-done.8), channel_id=1, source_target_pairs={{0,2},{2,4},{4,6},{6,8},{8,10},{10,12},{12,14},{14,16},{16,18},{18... | collective-permute-start | bytes 2654216 | tf_op jit(solution)/shard_map/ppermute | solution.py:21
  437.2 25.3 %collective-permute-start.10 = (bf16[144,3,1024]{2,0,1:T(8,128)(2,1)S(1)}, bf16[144,3,1024]{2,0,1:T(8,128)(2,1)S(1)}, u32[]{:S(2)}, u32[]{:S(2)}) collective-permute-start(bf16[144,3,1024]{2,0,1:T(8,128)(2,1)S(1)} %collective-permute-done.9), channel_id=1, source_target_pairs={{0,2},{2,4},{4,6},{6,8},{8,10},{10,12},{12,14},{14,16},{16,18},{18... | collective-permute-start | bytes 2654216 | tf_op jit(solution)/shard_map/ppermute | solution.py:21
  462.5 25.3 %collective-permute-start.11 = (bf16[144,3,1024]{2,0,1:T(8,128)(2,1)S(1)}, bf16[144,3,1024]{2,0,1:T(8,128)(2,1)S(1)}, u32[]{:S(2)}, u32[]{:S(2)}) collective-permute-start(bf16[144,3,1024]{2,0,1:T(8,128)(2,1)S(1)} %collective-permute-done.10), channel_id=1, source_target_pairs={{0,2},{2,4},{4,6},{6,8},{8,10},{10,12},{12,14},{14,16},{16,18},{18... | collective-permute-start | bytes 2654216 | tf_op jit(solution)/shard_map/ppermute | solution.py:21
  488.8 23.9 %collective-permute-start.12 = (bf16[144,3,1024]{2,0,1:T(8,128)(2,1)S(1)}, bf16[144,3,1024]{2,0,1:T(8,128)(2,1)}, u32[]{:S(2)}, u32[]{:S(2)}) collective-permute-start(bf16[144,3,1024]{2,0,1:T(8,128)(2,1)S(1)} %collective-permute-done.11), channel_id=1, source_target_pairs={{0,2},{2,4},{4,6},{6,8},{8,10},{10,12},{12,14},{14,16},{16,18},{18... | collective-permute-start | bytes 2654216 | tf_op jit(solution)/shard_map/ppermute | solution.py:21
  512.7 23.3 %collective-permute-start.13 = (bf16[144,3,1024]{2,0,1:T(8,128)(2,1)}, bf16[144,3,1024]{2,0,1:T(8,128)(2,1)}, u32[]{:S(2)}, u32[]{:S(2)}) collective-permute-start(bf16[144,3,1024]{2,0,1:T(8,128)(2,1)} %collective-permute-done.12), channel_id=1, source_target_pairs={{0,2},{2,4},{4,6},{6,8},{8,10},{10,12},{12,14},{14,16},{16,18},{18... | collective-permute-start | bytes 2654216 | tf_op jit(solution)/shard_map/ppermute | solution.py:21
  536.0 22.5 %collective-permute-start.14 = (bf16[144,3,1024]{2,0,1:T(8,128)(2,1)}, bf16[144,3,1024]{2,0,1:T(8,128)(2,1)}, u32[]{:S(2)}, u32[]{:S(2)}) collective-permute-start(bf16[144,3,1024]{2,0,1:T(8,128)(2,1)} %collective-permute-done.13), channel_id=1, source_target_pairs={{0,2},{2,4},{4,6},{6,8},{8,10},{10,12},{12,14},{14,16},{16,18},{18... | collective-permute-start | bytes 2654216 | tf_op jit(solution)/shard_map/ppermute | solution.py:21
  558.5 17.0 %collective-permute-start.15 = (bf16[144,3,1024]{2,0,1:T(8,128)(2,1)}, bf16[144,3,1024]{2,0,1:T(8,128)(2,1)S(1)}, u32[]{:S(2)}, u32[]{:S(2)}) collective-permute-start(bf16[144,3,1024]{2,0,1:T(8,128)(2,1)} %collective-permute-done.14), channel_id=1, source_target_pairs={{0,2},{2,4},{4,6},{6,8},{8,10},{10,12},{12,14},{14,16},{16,18},{18... | collective-permute-start | bytes 2654216 | tf_op jit(solution)/shard_map/ppermute | solution.py:21
  657.8 92.8 %all-to-all-start.3 = ((bf16[16,2,73728]{2,1,0:T(2,128)(2,1)}), bf16[16,2,73728]{2,1,0:T(2,128)(2,1)}, u32[]{:S(2)}, u32[]{:S(2)}) async-start(bf16[16,2,73728]{2,1,0:T(2,128)(2,1)} %reshape.255), calls=%async_computation.3 | async-start | bytes 9437184 | tf_op jit(solution)/shard_map/all_to_all | solution.py:80
  663.2 29.5 %all-reduce.8.cloned.1.call-start = ((), (), s32[]{:S(2)}) async-start(), calls=%async_computation.7 | async-start | bytes 1048576 | tf_op jit(solution)/shard_map/psum | solution.py:176
  750.6 44.3 %all-to-all-start.1 = ((bf16[16,2,16384]{2,1,0:T(2,128)(2,1)}), bf16[16,2,16384]{2,1,0:T(2,128)(2,1)S(1)}, u32[]{:S(2)}, u32[]{:S(2)}) async-start(bf16[16,2,16384]{2,1,0:T(2,128)(2,1)} %reshape.253), calls=%async_computation.1 | async-start | bytes 2097152 | tf_op jit(solution)/shard_map/all_to_all | solution.py:80
  754.3 8.7 collective-permute-start.17
  764.7 16.1 %collective-permute-start.16 = (bf16[1,2,1024]{2,1,0:T(2,128)(2,1)S(1)}, bf16[1,2,1024]{2,1,0:T(2,128)(2,1)S(1)}, u32[]{:S(2)}, u32[]{:S(2)}) collective-permute-start(bf16[1,2,1024]{2,1,0:T(2,128)(2,1)S(1)} %slice.144), channel_id=1, source_target_pairs={{2,0},{4,2},{6,4},{3,1},{5,3},{7,5},{10,8},{12,10},{14,12},{11,9},... | collective-permute-start | bytes 12296 | tf_op jit(solution)/shard_map/ppermute | solution.py:29
  794.9 97.1 %all-to-all-start = ((bf16[1,512,3,1024]{3,2,0,1:T(4,128)(2,1)}), bf16[1,512,3,1024]{3,2,0,1:T(4,128)(2,1)}, u32[]{:S(2)}, u32[]{:S(2)}) async-start(bf16[1,512,3,1024]{3,2,0,1:T(4,128)(2,1)} %copy.54), calls=%async_computation | async-start | bytes 8388608 | tf_op jit(solution)/shard_map/all_to_all | solution.py:73
  892.0 272.5 %all-to-all-start.2 = ((bf16[1,2304,2,1024]{3,2,0,1:T(2,128)(2,1)}), bf16[1,2304,2,1024]{3,2,0,1:T(2,128)(2,1)}, u32[]{:S(2)}, u32[]{:S(2)}) async-start(bf16[1,2304,2,1024]{3,2,0,1:T(2,128)(2,1)} %copy.59), calls=%async_computation.2 | async-start | bytes 18874368 | tf_op jit(solution)/shard_map/all_to_all | solution.py:73
  896.8 33.7 %all-reduce.10.cloned.1.call-start = ((), (), s32[]{:S(2)}) async-start(), calls=%async_computation.8 | async-start | bytes 1048576 | tf_op jit(solution)/shard_map/psum | solution.py:157
  925.1 218.6 %copy-start.43 = (f32[2,1024]{1,0:T(2,128)S(1)}, f32[2,1024]{1,0:T(2,128)}, u32[]{:S(2)}) copy-start(f32[2,1024]{1,0:T(2,128)} %param.19) | copy-start | bytes 24580
  925.1 219.2 %copy-start.42 = (f32[3,1024]{1,0:T(4,128)S(1)}, f32[3,1024]{1,0:T(4,128)}, u32[]{:S(2)}) copy-start(f32[3,1024]{1,0:T(4,128)} %param.18) | copy-start | bytes 36868
  925.2 219.2 %copy-start.51 = (f32[3,1024]{1,0:T(4,128)S(1)}, f32[3,1024]{1,0:T(4,128)}, u32[]{:S(2)}) copy-start(f32[3,1024]{1,0:T(4,128)} %param.24) | copy-start | bytes 36868
  925.2 219.2 %copy-start.52 = (f32[3,1024]{1,0:T(4,128)S(1)}, f32[3,1024]{1,0:T(4,128)}, u32[]{:S(2)}) copy-start(f32[3,1024]{1,0:T(4,128)} %param.25) | copy-start | bytes 36868
  925.2 221.6 %copy-start.4 = (f32[128,1024]{1,0:T(8,128)S(1)}, f32[128,1024]{1,0:T(8,128)}, u32[]{:S(2)}) copy-start(f32[128,1024]{1,0:T(8,128)} %copy-done.3) | copy-start | bytes 1572868
  (63 other events, 2080.7 us)
Sparse Core Ops, SparseCore 0:
  11.4 78.1 all-gather.2
  96.8 17.1 all-reduce.5
  117.5 260.7 all-gather.4
  672.8 19.8 all-reduce.7
  902.5 19.8 all-reduce.9
